TPU v7x, 256 devices: a whole 4x4x8 slice. The times are simulated.
256 devices in a mesh: mon: 64 (over y, z, core), out: 4 (over x).
Axes of the slice: x: 4, y: 4, z: 8, core: 2. Of those that a mesh axis runs over, the one named last changes fastest.
Arguments:
- mon_flow: bfloat16 [24576, 128], P('mon'), may hold values from -2.5 to 2.5
- out_flow: bfloat16 [4, 4096, 128], P('out', 'mon'), may hold values from -2.5 to 2.5
- rating: float32 [24576], P('mon'), may hold values from 1 to 3
- weights: float32 [128], replicated, may hold values from 0.25 to 1
- lodf: bfloat16 [64, 4, 8, 128, 128], P('mon', 'out'), may hold values from -1 to 1
- tile_mon: int32 [64, 4, 8], P('mon', 'out'), may hold values from 0 to 2
- tile_out: int32 [64, 4, 8], P('mon', 'out'), may hold values from 0 to 31
- tile_count: int32 [64, 4], P('mon', 'out'), may hold values from 1 to 8, as said below
Outputs:
- grad_mon: float32 [24576, 128], P(('mon', 'out'))
- grad_out: float32 [4, 4096, 128], P('out', 'mon')
Inputs may be any that keep to these rules, and one draw needn't show every extreme that they name: `tile_count`: each device has 1 to 8 live slots; some device has exactly 8 in every draw.
All inputs are finite; a program needn't handle non-finite values.
Results may differ from a plain program's by a relative error of at most 0.00085.
Values may be sent and summed in bfloat16 or wider, within the bound.
A program may use at most 64 MiB of HBM per device.

v0:
```python
import jax
import jax.numpy as jnp
from jax import lax
from jax.sharding import PartitionSpec as P


def tile_grads(lodf_tile, mon_block, out_block, rating_rows, weights):
    coupling = lodf_tile.astype(jnp.float32)
    post_flow = (
        mon_block.astype(jnp.float32)[:, None, :]
        + coupling[:, :, None] * out_block.astype(jnp.float32)[None, :, :]
    )
    inverse = 1.0 / (rating_rows * rating_rows)
    excess = post_flow * post_flow * inverse[:, None, None] - 1.0
    derivative = jax.nn.softplus(excess) * jax.nn.sigmoid(excess) * post_flow
    derivative = (
        derivative * (4.0 / coupling.shape[0]) * inverse[:, None, None] * weights[None, None, :]
    )
    return (jnp.sum(derivative, axis=1), jnp.sum(coupling[:, :, None] * derivative, axis=0))


def local(mon_flow, out_flow, rating, weights, lodf, tile_mon, tile_out, tile_count):
    width = lodf.shape[-1]
    scen = mon_flow.shape[1]
    gathered = lax.all_gather(out_flow, "mon", axis=1, tiled=True)[0]
    outage_blocks = gathered.reshape(-1, width, scen)
    mon_start = jnp.zeros(mon_flow.shape, jnp.float32)
    out_start = jnp.zeros(outage_blocks.shape, jnp.float32)

    def one_tile(mon_part, lodf_tile, mon_index, out_block):
        start = mon_index * width
        mon_rows = lax.dynamic_slice_in_dim(mon_flow, start, width, 0)
        rating_rows = lax.dynamic_slice_in_dim(rating, start, width, 0)
        grad_m, grad_k = tile_grads(lodf_tile, mon_rows, out_block, rating_rows, weights)
        old_rows = lax.dynamic_slice_in_dim(mon_part, start, width, 0)
        return (lax.dynamic_update_slice_in_dim(mon_part, old_rows + grad_m, start, 0), grad_k)

    def own_tile(slot_index, totals):
        mon_part, out_part = totals
        out_index = tile_out[0, 0, slot_index]
        mon_part, grad_k = one_tile(
            mon_part, lodf[0, 0, slot_index], tile_mon[0, 0, slot_index], outage_blocks[out_index]
        )
        old_block = lax.dynamic_index_in_dim(out_part, out_index, 0, keepdims=False)
        out_part = lax.dynamic_update_index_in_dim(out_part, old_block + grad_k, out_index, 0)
        return (mon_part, out_part)

    own_count = tile_count[0, 0]
    mon_part, out_part = lax.fori_loop(0, own_count, own_tile, (mon_start, out_start))
    grad_mon = lax.psum_scatter(mon_part, "out", scatter_dimension=0, tiled=True)
    grad_out = lax.psum_scatter(
        out_part.reshape(1, -1, scen), "mon", scatter_dimension=1, tiled=True
    )
    return (grad_mon, grad_out)


def solution(mesh):
    in_specs = (
        P("mon", None),
        P("out", "mon", None),
        P("mon"),
        P(),
        P("mon", "out", None, None, None),
        P("mon", "out", None),
        P("mon", "out", None),
        P("mon", "out"),
    )
    out_specs = (P(("mon", "out"), None), P("out", "mon", None))
    return jax.shard_map(local, mesh=mesh, in_specs=in_specs, out_specs=out_specs, check_vma=False)
```

profile of v0, /device:TPU:4, one launch (start us, length us, event | category | flops | bytes accessed | tf_op | source)
XLA Modules:
  0.0 414.8 jit_solution(17934352737875300077)
XLA Ops:
  7.2 0.7 all-gather.2.cloned.1.call-update
  8.0 82.2 %all-gather.2.cloned.1.call-done = bf16[1,4096,128]{2,1,0:T(8,128)(2,1)} async-done(((bf16[1,64,128]{2,1,0:T(8,128)(2,1)}), bf16[1,4096,128]{2,1,0:T(8,128)(2,1)}) %all-gather.2.cloned.1.call-update) | async-done | bytes 1048592 | tf_op jit(solution)/shard_map/all_gather | solution.py:25
  90.4 57.0 %while.14 = (s32[]{:T(128)}, f32[384,128]{1,0:T(8,128)S(1)}, f32[32,128,128]{2,1,0:T(8,128)S(1)}, s32[]{:T(128)}, s32[1,1,8]{2,1,0:T(1,128)S(1)}, /*index=5*/bf1...) while((s32[]{:T(128)}, f32[384,128]{1,0:T(8,128)S(1)}, ...), condition=%wide.region_3.4_spmd, body=%wide.region_0.3_spmd.sunk | while | flops 44089740 | bytes 1019183 | solution.py:49
  91.1 0.6 constant_dynamic-slice_fusion.3
  95.6 0.8 broadcast_multiply_fusion.2
  96.3 0.8 bitcast_convert_fusion.4
  97.1 0.8 dynamic-slice_convert_fusion.2
  97.9 0.8 bitcast_convert_fusion.5
  98.6 10.5 %multiply_reduce_fusion.2 = (f32[128,128]{1,0:T(8,128)S(1)}, f32[128,128]{1,0:T(8,128)S(1)}) fusion(f32[128,128]{1,0:T(8,128)S(1)} %bitcast_convert_fusion.4, f32[128]{0:T(128)S(1)} %get-tuple-element.295, f32[128]{0:T(128)S(1)} %get-tuple-element.248, f32[128]{0:T(128)S(1)} %get-tuple-element.249, f32[128,128]{1,0:T(8,128)S(1)} %bitcast_convert_fusion.5, ...), kind=kLoop, calls=%fused_computation.5.clone.1 | loop fusion | flops 44007424 | bytes 329216 | tf_op jit(solution)/shard_map/while/body/reduce_sum | solution.py:19
  114.4 0.8 broadcast_multiply_fusion.2
  115.1 0.8 bitcast_convert_fusion.4
  115.9 0.8 dynamic-slice_convert_fusion.2
  116.6 0.8 bitcast_convert_fusion.5
  117.4 10.5 %multiply_reduce_fusion.2 = (f32[128,128]{1,0:T(8,128)S(1)}, f32[128,128]{1,0:T(8,128)S(1)}) fusion(f32[128,128]{1,0:T(8,128)S(1)} %bitcast_convert_fusion.4, f32[128]{0:T(128)S(1)} %get-tuple-element.295, f32[128]{0:T(128)S(1)} %get-tuple-element.248, f32[128]{0:T(128)S(1)} %get-tuple-element.249, f32[128,128]{1,0:T(8,128)S(1)} %bitcast_convert_fusion.5, ...), kind=kLoop, calls=%fused_computation.5.clone.1 | loop fusion | flops 44007424 | bytes 329216 | tf_op jit(solution)/shard_map/while/body/reduce_sum | solution.py:19
  128.7 0.6 constant_dynamic-slice_fusion.3
  133.1 0.8 broadcast_multiply_fusion.2
  133.9 0.8 bitcast_convert_fusion.4
  134.7 0.8 dynamic-slice_convert_fusion.2
  135.4 0.8 bitcast_convert_fusion.5
  136.2 10.5 %multiply_reduce_fusion.2 = (f32[128,128]{1,0:T(8,128)S(1)}, f32[128,128]{1,0:T(8,128)S(1)}) fusion(f32[128,128]{1,0:T(8,128)S(1)} %bitcast_convert_fusion.4, f32[128]{0:T(128)S(1)} %get-tuple-element.295, f32[128]{0:T(128)S(1)} %get-tuple-element.248, f32[128]{0:T(128)S(1)} %get-tuple-element.249, f32[128,128]{1,0:T(8,128)S(1)} %bitcast_convert_fusion.5, ...), kind=kLoop, calls=%fused_computation.5.clone.1 | loop fusion | flops 44007424 | bytes 329216 | tf_op jit(solution)/shard_map/while/body/reduce_sum | solution.py:19
  147.5 0.6 copy-done.1
  148.2 0.7 copy-done
  148.9 112.1 %reduce-scatter.3.cloned.1.call-done = f32[96,128]{1,0:T(8,128)} async-done(((f32[384,128]{1,0:T(8,128)}), f32[96,128]{1,0:T(8,128)}) %reduce-scatter.3.cloned.1.call-update) | async-done | bytes 49168 | tf_op jit(solution)/shard_map/reduce_scatter | solution.py:50
  261.0 147.2 %reduce-scatter.5.cloned.1.call-done = f32[1,64,128]{2,1,0:T(8,128)} async-done(((f32[1,4096,128]{2,1,0:T(8,128)}), f32[1,64,128]{2,1,0:T(8,128)}) %reduce-scatter.5.cloned.1.call-update) | async-done | bytes 32784 | tf_op jit(solution)/shard_map/reduce_scatter | solution.py:51
  (22 shorter events, 1.1 us)
Async XLA Ops:
  7.2 83.2 %copy-start.3 = (s32[1,1,8]{2,1,0:T(1,128)S(1)}, s32[1,1,8]{2,1,0:T(1,128)}, u32[]{:S(2)}) copy-start(s32[1,1,8]{2,1,0:T(1,128)} %param.16) | copy-start | bytes 100
  7.2 83.2 %copy-start.2 = (s32[1,1,8]{2,1,0:T(1,128)S(1)}, s32[1,1,8]{2,1,0:T(1,128)}, u32[]{:S(2)}) copy-start(s32[1,1,8]{2,1,0:T(1,128)} %param.15) | copy-start | bytes 100
  7.2 83.2 %copy-start.4 = (f32[128]{0:T(128)S(1)}, f32[128]{0:T(128)}, u32[]{:S(2)}) copy-start(f32[128]{0:T(128)} %param.13) | copy-start | bytes 1540
  7.2 83.0 %all-gather.2.cloned.1.call-start = ((), (), s32[]{:S(2)}) async-start(), calls=%async_computation.2 | async-start | bytes 1064960 | tf_op jit(solution)/shard_map/all_gather | solution.py:25
  7.9 253.1 %reduce-scatter.3.cloned.1.call-start = ((), (), s32[]{:S(2)}) async-start(), calls=%async_computation.3 | async-start | bytes 245760 | tf_op jit(solution)/shard_map/reduce_scatter | solution.py:50
  147.5 0.7 copy-start.1
  147.5 1.4 copy-start
  148.1 260.1 %reduce-scatter.5.cloned.1.call-start = ((), (), s32[]{:S(2)}) async-start(), calls=%async_computation.4 | async-start | bytes 2129920 | tf_op jit(solution)/shard_map/reduce_scatter | solution.py:51
Sparse Core Ops, SparseCore 0:
  10.8 79.3 all-gather.1
  148.3 112.7 reduce-scatter.2
  266.2 142.0 reduce-scatter.4
where the time goes:
time: 417 us; the launch traced here: 415 us
  waiting for transfers between devices  342 us (82%)
  other arithmetic  42.7 us (10%)
  loops' own time  14.3 us (3%)
  between operations  13.8 us (3%)
    reduce_scatter x1, waiting for transfers between devices, local(): lax.psum_scatter(out_part.reshape(1, -1, scen), 'mon', scatter_dimension=...  147 us
    reduce_scatter x1, waiting for transfers between devices, local(): lax.psum_scatter(mon_part, 'out', scatter_dimension=0, tiled=True)  112 us
    all_gather x1, waiting for transfers between devices, local(): gathered = lax.all_gather(out_flow, 'mon', axis=1, tiled=True)[0]  82.2 us
    reduce_sum x3, other arithmetic, tile_grads(): jnp.sum(coupling[:, :, None] * derivative, axis=0)  31.6 us
    another operation x1, loops' own time, local(): lax.fori_loop(0, own_count, own_tile, (mon_start, out_start))  14.3 us
  transfers between devices with their start and end apart: 3, of which 3 were waited for; matrix products, arithmetic and copies ran while one was open for 0% of the time, Pallas kernels for 0%

commit v1 on v0

--- a/solution.py
+++ b/solution.py
@@ -22,7 +22,9 @@
 def local(mon_flow, out_flow, rating, weights, lodf, tile_mon, tile_out, tile_count):
     width = lodf.shape[-1]
     scen = mon_flow.shape[1]
-    gathered = lax.all_gather(out_flow, "mon", axis=1, tiled=True)[0]
+    gathered = jnp.concatenate(
+        lax.all_to_all(jnp.stack([out_flow] * lax.axis_size("mon")), "mon", 0, 0), axis=1
+    )[0]
     outage_blocks = gathered.reshape(-1, width, scen)
     mon_start = jnp.zeros(mon_flow.shape, jnp.float32)
     out_start = jnp.zeros(outage_blocks.shape, jnp.float32)

time: 417 us -> 367 us (0.88)
  waiting for transfers between devices: 342 us -> 281 us
  starting transfers between devices: 0.12 us -> 12.3 us
    all_gather x1 -> x0, waiting for transfers between devices: 82.2 us -> none  [local(): gathered = lax.all_gather(out_flow, 'mon', axis=1, tiled=True)[0]]
    all_to_all x0 -> x1, waiting for transfers between devices: none -> 28.1 us  [local(): lax.all_to_all(jnp.stack([out_flow] * lax.axis_size('mon')), 'mon', 0, 0)]
    all_to_all x0 -> x1, starting transfers between devices: none -> 12.2 us  [local(): lax.all_to_all(jnp.stack([out_flow] * lax.axis_size('mon')), 'mon', 0, 0)]
    reduce_scatter x1, waiting for transfers between devices: 112 us -> 106 us  [local(): lax.psum_scatter(mon_part, 'out', scatter_dimension=0, tiled=True)]
where the time goes in v1:
time: 367 us; the launch traced here: 365 us
  waiting for transfers between devices  281 us (77%)
  other arithmetic  40.4 us (11%)
  between operations  14.1 us (4%)
  loops' own time  13.6 us (4%)
  starting transfers between devices  12.3 us (3%)
    reduce_scatter x1, waiting for transfers between devices, local(): lax.psum_scatter(out_part.reshape(1, -1, scen), 'mon', scatter_dimension=...  147 us
    reduce_scatter x1, waiting for transfers between devices, local(): lax.psum_scatter(mon_part, 'out', scatter_dimension=0, tiled=True)  106 us
    reduce_sum x3, other arithmetic, tile_grads(): jnp.sum(coupling[:, :, None] * derivative, axis=0)  31.7 us
    all_to_all x1, waiting for transfers between devices, local(): lax.all_to_all(jnp.stack([out_flow] * lax.axis_size('mon')), 'mon', 0, 0)  28.1 us
    another operation x1, loops' own time, local(): lax.fori_loop(0, own_count, own_tile, (mon_start, out_start))  13.6 us
    all_to_all x1, starting transfers between devices, local(): lax.all_to_all(jnp.stack([out_flow] * lax.axis_size('mon')), 'mon', 0, 0)  12.2 us
  transfers between devices with their start and end apart: 3, of which 3 were waited for; matrix products, arithmetic and copies ran while one was open for 0% of the time, Pallas kernels for 0%

profile of v1, /device:TPU:4, one launch (start us, length us, event | category | flops | bytes accessed | tf_op | source)
XLA Modules:
  0.0 365.4 jit_solution(6838186443128524246)
XLA Ops:
  7.2 1.9 stack.2
  9.1 12.2 %all-to-all-start = ((bf16[64,1,64,128]{3,2,1,0:T(8,128)(2,1)}), bf16[64,1,64,128]{3,2,1,0:T(8,128)(2,1)S(1)}, u32[]{:S(2)}, u32[]{:S(2)}) async-start(bf16[64,1,64,128]{3,2,1,0:T(8,128)(2,1)} %stack.2), calls=%async_computation | async-start | bytes 2097152 | tf_op jit(solution)/shard_map/all_to_all | solution.py:26
  21.4 28.1 %all-to-all-done = bf16[64,1,64,128]{3,2,1,0:T(8,128)(2,1)S(1)} async-done(((bf16[64,1,64,128]{3,2,1,0:T(8,128)(2,1)}), bf16[64,1,64,128]{3,2,1,0:T(8,128)(2,1)S(1)}, u32[]{:S(2)}, u32[]{:S(2)}) %all-to-all-start) | async-done | bytes 1048608 | tf_op jit(solution)/shard_map/all_to_all | solution.py:26
  49.6 0.2 broadcast_in_dim.6
  49.8 54.0 %while.14 = (s32[]{:T(128)}, f32[384,128]{1,0:T(8,128)S(1)}, f32[32,128,128]{2,1,0:T(8,128)S(1)}, s32[]{:T(128)}, s32[1,1,8]{2,1,0:T(1,128)S(1)}, /*index=5*/bf1...) while((s32[]{:T(128)}, f32[384,128]{1,0:T(8,128)S(1)}, ...), condition=%wide.region_3.4_spmd, body=%wide.region_0.3_spmd.sunk | while | flops 44089740 | bytes 1019183 | solution.py:51
  50.5 0.6 constant_dynamic-slice_fusion.3
  54.7 0.8 broadcast_multiply_fusion.2
  55.5 0.8 bitcast_convert_fusion.4
  56.2 0.8 dynamic-slice_convert_fusion.2
  57.0 10.6 %multiply_reduce_fusion.2 = (f32[128,128]{1,0:T(8,128)S(1)}, f32[128,128]{1,0:T(8,128)S(1)}) fusion(f32[128,128]{1,0:T(8,128)S(1)} %bitcast_convert_fusion.4, f32[128]{0:T(128)S(1)} %get-tuple-element.295, f32[128]{0:T(128)S(1)} %get-tuple-element.248, f32[128]{0:T(128)S(1)} %get-tuple-element.249, f32[128,128]{1,0:T(8,128)S(1)} %bitcast_convert_fusion.5, ...), kind=kLoop, calls=%fused_computation.5.clone.1 | loop fusion | flops 44007424 | bytes 329216 | tf_op jit(solution)/shard_map/while/body/reduce_sum | solution.py:19
  68.3 0.6 constant_dynamic-slice_fusion.3
  72.5 0.8 broadcast_multiply_fusion.2
  73.3 0.8 bitcast_convert_fusion.4
  74.0 0.8 dynamic-slice_convert_fusion.2
  74.8 10.6 %multiply_reduce_fusion.2 = (f32[128,128]{1,0:T(8,128)S(1)}, f32[128,128]{1,0:T(8,128)S(1)}) fusion(f32[128,128]{1,0:T(8,128)S(1)} %bitcast_convert_fusion.4, f32[128]{0:T(128)S(1)} %get-tuple-element.295, f32[128]{0:T(128)S(1)} %get-tuple-element.248, f32[128]{0:T(128)S(1)} %get-tuple-element.249, f32[128,128]{1,0:T(8,128)S(1)} %bitcast_convert_fusion.5, ...), kind=kLoop, calls=%fused_computation.5.clone.1 | loop fusion | flops 44007424 | bytes 329216 | tf_op jit(solution)/shard_map/while/body/reduce_sum | solution.py:19
  86.1 0.6 constant_dynamic-slice_fusion.3
  90.3 0.8 broadcast_multiply_fusion.2
  91.1 0.8 bitcast_convert_fusion.4
  91.8 0.8 dynamic-slice_convert_fusion.2
  92.6 10.6 %multiply_reduce_fusion.2 = (f32[128,128]{1,0:T(8,128)S(1)}, f32[128,128]{1,0:T(8,128)S(1)}) fusion(f32[128,128]{1,0:T(8,128)S(1)} %bitcast_convert_fusion.4, f32[128]{0:T(128)S(1)} %get-tuple-element.295, f32[128]{0:T(128)S(1)} %get-tuple-element.248, f32[128]{0:T(128)S(1)} %get-tuple-element.249, f32[128,128]{1,0:T(8,128)S(1)} %bitcast_convert_fusion.5, ...), kind=kLoop, calls=%fused_computation.5.clone.1 | loop fusion | flops 44007424 | bytes 329216 | tf_op jit(solution)/shard_map/while/body/reduce_sum | solution.py:19
  103.9 0.7 copy-done.1
  104.6 0.6 copy-done
  105.3 105.9 %reduce-scatter.3.cloned.1.call-done = f32[96,128]{1,0:T(8,128)} async-done(((f32[384,128]{1,0:T(8,128)}), f32[96,128]{1,0:T(8,128)}) %reduce-scatter.3.cloned.1.call-update) | async-done | bytes 49168 | tf_op jit(solution)/shard_map/reduce_scatter | solution.py:52
  211.2 147.3 %reduce-scatter.5.cloned.1.call-done = f32[1,64,128]{2,1,0:T(8,128)} async-done(((f32[1,4096,128]{2,1,0:T(8,128)}), f32[1,64,128]{2,1,0:T(8,128)}) %reduce-scatter.5.cloned.1.call-update) | async-done | bytes 32784 | tf_op jit(solution)/shard_map/reduce_scatter | solution.py:53
  (22 shorter events, 0.3 us)
Async XLA Ops:
  9.1 40.7 %copy-start.2 = (s32[1,1,8]{2,1,0:T(1,128)S(1)}, s32[1,1,8]{2,1,0:T(1,128)}, u32[]{:S(2)}) copy-start(s32[1,1,8]{2,1,0:T(1,128)} %param.15) | copy-start | bytes 100
  9.1 40.7 %copy-start.3 = (s32[1,1,8]{2,1,0:T(1,128)S(1)}, s32[1,1,8]{2,1,0:T(1,128)}, u32[]{:S(2)}) copy-start(s32[1,1,8]{2,1,0:T(1,128)} %param.16) | copy-start | bytes 100
  9.1 40.7 %copy-start.4 = (f32[128]{0:T(128)S(1)}, f32[128]{0:T(128)}, u32[]{:S(2)}) copy-start(f32[128]{0:T(128)} %param.13) | copy-start | bytes 1540
  9.1 40.4 %all-to-all-start = ((bf16[64,1,64,128]{3,2,1,0:T(8,128)(2,1)}), bf16[64,1,64,128]{3,2,1,0:T(8,128)(2,1)S(1)}, u32[]{:S(2)}, u32[]{:S(2)}) async-start(bf16[64,1,64,128]{3,2,1,0:T(8,128)(2,1)} %stack.2), calls=%async_computation | async-start | bytes 2097152 | tf_op jit(solution)/shard_map/all_to_all | solution.py:26
  21.4 189.9 %reduce-scatter.3.cloned.1.call-start = ((), (), s32[]{:S(2)}) async-start(), calls=%async_computation.3 | async-start | bytes 245760 | tf_op jit(solution)/shard_map/reduce_scatter | solution.py:52
  103.9 0.7 copy-start.1
  103.9 1.4 copy-start
  104.6 253.9 %reduce-scatter.5.cloned.1.call-start = ((), (), s32[]{:S(2)}) async-start(), calls=%async_computation.4 | async-start | bytes 2129920 | tf_op jit(solution)/shard_map/reduce_scatter | solution.py:53
Sparse Core Ops, SparseCore 0:
  104.7 106.4 reduce-scatter.2
  216.4 142.0 reduce-scatter.4
